TPU v7x, 32 devices: a whole 2x2x4 slice. The times are simulated.
32 devices in a mesh: groups: 2 (over y), seq: 8 (over z, x), tensor: 2 (over core).
Axes of the slice: x: 2, y: 2, z: 4, core: 2. Of those that a mesh axis runs over, the one named last changes fastest.
Arguments:
- queries: bfloat16 [2048, 1536], P(('groups', 'seq'), 'tensor'), parts along dimension 0, may hold values from -64 to 64
- keys: bfloat16 [2048, 1536], P(('groups', 'seq'), 'tensor'), parts along dimension 0, may hold values from -6 to 6
- values: bfloat16 [2048, 1536], P(('groups', 'seq'), 'tensor'), parts along dimension 0, may hold values from -6 to 6
- text_keys: bfloat16 [64, 1536], P(('groups', 'seq'), 'tensor'), parts along dimension 0, may hold values from -6 to 6
- text_values: bfloat16 [64, 1536], P(('groups', 'seq'), 'tensor'), parts along dimension 0, may hold values from -6 to 6
- conv_weight: bfloat16 [4, 1536], P(None, 'tensor'), may hold values from -3 to 3
- out_weight: bfloat16 [1536, 1536], P('tensor'), may hold values from -0.15625 to 0.15625
- image_hidden: bfloat16 [2048, 1536], P(('groups', 'seq')), parts along dimension 0, may hold values from -6 to 6
- gate: bfloat16 [3072], P('groups'), parts along dimension 0, may hold values from -8 to 8
Outputs:
- mixed: bfloat16 [2048, 1536], P(('groups', 'seq')), parts along dimension 0
There are 2 independent parts, one for each index of `groups`. A program takes and returns all parts, laid end to end along the dimension named above; an argument that names none is the same for every part. Nothing has to cross between parts.
All inputs are finite; a program needn't handle non-finite values.
Results may differ from a plain program's by a relative error of at most 0.011.
Values may be sent and summed in bfloat16 or wider, within the bound.
A program may use at most 64 MiB of HBM per device.

v0:
```python
import math
import jax
import jax.numpy as jnp
from jax import lax
from jax.sharding import PartitionSpec as P

HEAD_DIM = 128
key_block = 512


def rope_angles(row_pos, col_pos, head_dim):
    lead_dims = head_dim // 8
    group_dims = head_dim * 7 // 16
    frequency = 10000.0 ** (-(2.0 * jnp.arange(group_dims // 2, dtype=jnp.float32)) / group_dims)
    zero_angles = jnp.zeros((row_pos.shape[0], lead_dims // 2), jnp.float32)
    return jnp.concatenate(
        [zero_angles, row_pos[:, None] * frequency[None, :], col_pos[:, None] * frequency[None, :]],
        axis=1,
    )


def apply_rope(field, angles):
    paired = field.reshape(field.shape[0], field.shape[1], field.shape[2] // 2, 2)
    even_part = paired[..., 0]
    odd_part = paired[..., 1]
    cos_part = jnp.cos(angles)[:, None, :]
    sin_part = jnp.sin(angles)[:, None, :]
    turned = jnp.stack(
        [even_part * cos_part - odd_part * sin_part, even_part * sin_part + odd_part * cos_part],
        axis=-1,
    )
    return turned.reshape(field.shape)


def compress(field, taps, row_width):
    features = field.shape[1]
    grid_cells = field.astype(jnp.float32).reshape(2, row_width // 2, 2, features)
    tap_grid = taps.astype(jnp.float32).reshape(2, 2, features)
    return (
        grid_cells[0, :, 0] * tap_grid[0, 0]
        + grid_cells[0, :, 1] * tap_grid[0, 1]
        + grid_cells[1, :, 0] * tap_grid[1, 0]
        + grid_cells[1, :, 1] * tap_grid[1, 1]
    )


def absorb_block(carry, key_rows, value_rows, queries_rot):
    row_max, row_total, accumulated = carry
    heads_dev = queries_rot.shape[1]
    key_heads = key_rows.reshape(key_rows.shape[0], heads_dev, -1)
    value_heads = value_rows.reshape(value_rows.shape[0], heads_dev, -1)
    scores = jnp.einsum(
        "qhd,khd->hqk", queries_rot, key_heads, preferred_element_type=jnp.float32
    ) * (1.0 / math.sqrt(HEAD_DIM))
    new_max = jnp.maximum(row_max, jnp.max(scores, axis=-1))
    rescale = jnp.exp(row_max - new_max)
    weights = jnp.exp(scores - new_max[:, :, None]).astype(jnp.bfloat16)
    row_total = row_total * rescale + jnp.sum(weights.astype(jnp.float32), axis=-1)
    mixed_values = jnp.einsum(
        "hqk,khd->qhd", weights, value_heads, preferred_element_type=jnp.float32
    )
    accumulated = accumulated * rescale.T[:, :, None] + mixed_values
    return (new_max, row_total, accumulated)


def absorb(carry, key_rows, value_rows, queries_rot):
    key_count = key_rows.shape[0]
    if key_count > key_block and key_count % key_block == 0:
        stacked_keys = key_rows.reshape(key_count // key_block, key_block, key_rows.shape[1])
        stacked_values = value_rows.reshape(key_count // key_block, key_block, value_rows.shape[1])

        def one_step(running, block_pair):
            return (absorb_block(running, block_pair[0], block_pair[1], queries_rot), None)

        carry, unused = lax.scan(one_step, carry, (stacked_keys, stacked_values))
        return carry
    return absorb_block(carry, key_rows, value_rows, queries_rot)


def local(
    queries, keys, values, text_keys, text_values, conv_weight, out_weight, image_hidden, gate
):
    local_tokens, features = queries.shape
    row_width = local_tokens // 2
    heads_dev = features // HEAD_DIM
    seq_place = lax.axis_index("seq").astype(jnp.float32)
    token_ids = jnp.arange(local_tokens, dtype=jnp.int32)
    query_rows = 2.0 * seq_place + (token_ids // row_width).astype(jnp.float32)
    query_cols = (token_ids % row_width).astype(jnp.float32)
    queries_rot = apply_rope(
        queries.astype(jnp.float32).reshape(local_tokens, heads_dev, HEAD_DIM),
        rope_angles(query_rows, query_cols, HEAD_DIM),
    ).astype(jnp.bfloat16)
    patch_ids = jnp.arange(row_width // 2, dtype=jnp.int32).astype(jnp.float32)
    patch_rows = 2.0 * seq_place + 0.5 + 0.0 * patch_ids
    patch_cols = 2.0 * patch_ids + 0.5
    short_keys = (
        apply_rope(
            compress(keys, conv_weight, row_width).reshape(row_width // 2, heads_dev, HEAD_DIM),
            rope_angles(patch_rows, patch_cols, HEAD_DIM),
        )
        .astype(jnp.bfloat16)
        .reshape(row_width // 2, features)
    )
    short_values = compress(values, conv_weight, row_width).astype(jnp.bfloat16)
    initial = (
        jnp.full((heads_dev, local_tokens), -1e30, jnp.float32),
        jnp.zeros((heads_dev, local_tokens), jnp.float32),
        jnp.zeros((local_tokens, heads_dev, HEAD_DIM), jnp.float32),
    )
    all_text_keys, all_text_values = (
        lax.all_gather(text_keys, "seq", axis=0, tiled=True),
        lax.all_gather(text_values, "seq", axis=0, tiled=True),
    )
    after_text = absorb(initial, all_text_keys, all_text_values, queries_rot)
    row_max, row_total, accumulated = absorb(
        after_text,
        lax.all_gather(short_keys, "seq", axis=0, tiled=True),
        lax.all_gather(short_values, "seq", axis=0, tiled=True),
        queries_rot,
    )
    attended = (
        (accumulated / row_total.T[:, :, None]).astype(jnp.bfloat16).reshape(local_tokens, features)
    )
    projected = lax.psum(
        jnp.dot(attended, out_weight, preferred_element_type=jnp.float32).astype(jnp.bfloat16),
        "tensor",
    ).astype(jnp.float32)
    return (
        image_hidden.astype(jnp.float32) + gate.astype(jnp.float32)[None, :] * projected
    ).astype(jnp.bfloat16)


def solution(mesh):
    placed = (
        P(("groups", "seq"), "tensor"),
        P(("groups", "seq"), "tensor"),
        P(("groups", "seq"), "tensor"),
        P(("groups", "seq"), "tensor"),
        P(("groups", "seq"), "tensor"),
        P(None, "tensor"),
        P("tensor", None),
        P(("groups", "seq"), None),
        P("groups"),
    )
    return jax.shard_map(
        local, mesh=mesh, in_specs=placed, out_specs=P(("groups", "seq"), None), check_vma=False
    )
```

profile of v0, /device:TPU:0, one launch (start us, length us, event | category | flops | bytes accessed | tf_op | source)
XLA Modules:
  0.0 191.8 jit_solution(10425235532652120512)
XLA Ops:
  7.1 0.6 fusion.22
  7.6 0.7 reshape.261
  8.4 0.8 mul.304
  9.2 0.8 mul.307
  10.1 0.8 mul.310
  10.9 0.8 mul.313
  11.7 1.1 reshape.259
  12.9 1.0 fusion.27
  14.2 1.1 copy.64
  15.2 1.8 copy.65
  17.0 0.6 fusion.24
  17.6 0.7 broadcast_multiply_fusion.1
  18.5 3.4 %multiply_add_fusion = f32[32,6,64,2]{0,3,2,1:T(2,128)S(1)} fusion(f32[32,6,64,2]{0,3,2,1:T(2,128)S(1)} %bitcast.86, f32[32,6,64,2]{0,3,2,1:T(2,128)} %bitcast.89, f32[32,6,64,2]{0,3,2,1:T(2,128)S(1)} %bitcast.88, f32[32,6,64,2]{0,3,2,1:T(2,128)S(1)} %bitcast.87, f32[6,64,2]{2,1,0:T(8,128)} %mul.313, f32[6,64,2]{2,1,0:T(8,128)} %mul.310, ...), kind=kLoop, calls=%fused_computation.13 | loop fusion | flops 172032 | bytes 503808 | tf_op jit(solution)/shard_map/add | solution.py:40
  22.5 0.5 pad_maximum_fusion.1
  23.1 32.8 %all_gather.14 = bf16[256,768]{1,0:T(8,128)(2,1)S(1)} all-gather(bf16[32,768]{1,0:T(8,128)(2,1)S(1)} %copy.51), channel_id=1, replica_groups=mesh['groups'=2,'seq'=8,'tensor'=2] {'seq'}, dimensions={0}, use_global_device_ids=true | all-gather | bytes 442368 | tf_op jit(solution)/shard_map/all_gather | solution.py:118
  56.4 31.0 %all-gather = bf16[8,4,768]{2,1,0:T(4,128)(2,1)S(1)} all-gather(bf16[1,4,768]{2,1,0:T(4,128)(2,1)} %bitcast.93), channel_id=1, replica_groups=mesh['groups'=2,'seq'=8,'tensor'=2] {'seq'}, dimensions={0}, use_global_device_ids=true | all-gather | bytes 55296 | tf_op jit(solution)/shard_map/all_gather | solution.py:112
  87.4 0.7 reshape.246
  88.0 0.8 broadcast_multiply_fusion.3
  88.8 0.8 fusion.17
  90.6 1.0 fusion.30
  91.5 1.4 fusion.29
  92.9 1.1 reshape.263
  94.4 31.0 %all_gather.15 = bf16[256,768]{1,0:T(8,128)(2,1)S(1)} all-gather(bf16[32,768]{1,0:T(8,128)(2,1)S(1)} %fusion.8), channel_id=1, replica_groups=mesh['groups'=2,'seq'=8,'tensor'=2] {'seq'}, dimensions={0}, use_global_device_ids=true | all-gather | bytes 442368 | tf_op jit(solution)/shard_map/all_gather | solution.py:119
  125.4 0.9 copy.58
  126.3 0.7 broadcast_maximum_fusion
  127.3 2.1 %convolution_bitcast_fusion.1 = f32[128,6,128]{0,2,1:T(8,128)} fusion(bf16[256,6,128]{0,2,1:T(8,128)(2,1)} %bitcast.85, f32[6,128,256]{2,1,0:T(8,128)S(1)} %get-tuple-element.37, f32[6,128]{1,0:T(8,128)S(1)} %get-tuple-element.29), kind=kOutput, calls=%fused_computation.4 | convolution fusion | flops 50724864 | bytes 1575936 | tf_op jit(solution)/shard_map/hqk,khd->qhd/dot_general | solution.py:59
  129.4 30.8 %all-gather.1 = bf16[8,4,768]{2,1,0:T(4,128)(2,1)S(1)} all-gather(bf16[1,4,768]{2,1,0:T(4,128)(2,1)S(1)} %bitcast.94), channel_id=1, replica_groups=mesh['groups'=2,'seq'=8,'tensor'=2] {'seq'}, dimensions={0}, use_global_device_ids=true | all-gather | bytes 55296 | tf_op jit(solution)/shard_map/all_gather | solution.py:113
  160.3 0.7 bitcast_add_fusion
  161.0 1.4 fusion.4
  162.4 1.2 convolution_convert_fusion
  163.7 19.4 %all-reduce.2.cloned.1.call-done = bf16[128,1536]{1,0:T(8,128)(2,1)} async-done(((bf16[128,1536]{1,0:T(8,128)(2,1)}), bf16[128,1536]{1,0:T(8,128)(2,1)}) %all-reduce.2.cloned.1.call-update) | async-done | bytes 393232 | tf_op jit(solution)/shard_map/psum | solution.py:125
  183.1 1.9 add_convert_fusion
  (39 shorter events, 4.0 us)
Async XLA Ops:
  6.5 155.8 %copy-start = (bf16[768,1536]{1,0:T(8,128)(2,1)S(1)}, bf16[768,1536]{1,0:T(8,128)(2,1)}, u32[]{:S(2)}) copy-start(bf16[768,1536]{1,0:T(8,128)(2,1)} %param.15) | copy-start | bytes 7077892
  6.5 176.6 %all-reduce.2.cloned.1.call-start = ((), (), s32[]{:S(2)}) async-start(), calls=%async_computation | async-start | bytes 786432 | tf_op jit(solution)/shard_map/psum | solution.py:125
  17.6 0.9 copy-start.7
  21.9 34.1 %copy-start.4 = (bf16[128,768]{1,0:T(8,128)(2,1)S(1)}, bf16[128,768]{1,0:T(8,128)(2,1)}, u32[]{:S(2)}) copy-start(bf16[128,768]{1,0:T(8,128)(2,1)} %param.9) | copy-start | bytes 589828
  88.0 3.5 %copy-start.3 = (bf16[32,6,128]{2,1,0:T(8,128)(2,1)S(1)}, bf16[32,6,128]{2,1,0:T(8,128)(2,1)}, u32[]{:S(2)}) copy-start(bf16[32,6,128]{2,1,0:T(8,128)(2,1)} %reshape.246) | copy-start | bytes 147460
  94.4 35.0 %copy-start.5 = (bf16[4,768]{1,0:T(4,128)(2,1)S(1)}, bf16[4,768]{1,0:T(4,128)(2,1)}, u32[]{:S(2)}) copy-start(bf16[4,768]{1,0:T(4,128)(2,1)} %param.13) | copy-start | bytes 18436
  126.3 33.9 %copy-start.2 = (f32[6,128,32]{1,2,0:T(8,128)S(1)}, f32[6,128,32]{1,2,0:T(8,128)}, u32[]{:S(2)}) copy-start(f32[6,128,32]{1,2,0:T(8,128)} %get-tuple-element.35) | copy-start | bytes 294916
  161.0 2.7 %copy-start.6 = (bf16[1536]{0:T(1024)(128)(2,1)S(1)}, bf16[1536]{0:T(1024)(128)(2,1)}, u32[]{:S(2)}) copy-start(bf16[1536]{0:T(1024)(128)(2,1)} %param.17) | copy-start | bytes 9220
  161.0 22.1 %copy-start.1 = (bf16[128,1536]{1,0:T(8,128)(2,1)S(1)}, bf16[128,1536]{1,0:T(8,128)(2,1)}, u32[]{:S(2)}) copy-start(bf16[128,1536]{1,0:T(8,128)(2,1)} %param.16) | copy-start | bytes 1179652
Sparse Core Ops, SparseCore 0:
  163.8 19.2 all-reduce.1
where the time goes:
time: 192 us
  blocking collectives  125 us (65%)
  waiting for transfers between devices  19.4 us (10%)
  between operations  13.6 us (7%)
  other arithmetic  13.3 us (7%)
  local copies, waits for them, and re-layouts  12.9 us (7%)
  matrix products  7.08 us (4%)
    all_gather x1, blocking collectives, local(): lax.all_gather(short_keys, 'seq', axis=0, tiled=True)  32.8 us
    all_gather x1, blocking collectives, local(): lax.all_gather(text_keys, 'seq', axis=0, tiled=True)  31 us
    all_gather x1, blocking collectives, local(): lax.all_gather(short_values, 'seq', axis=0, tiled=True)  31 us
    all_gather x1, blocking collectives, local(): lax.all_gather(text_values, 'seq', axis=0, tiled=True)  30.8 us
    psum x1, waiting for transfers between devices, local(): lax.psum(jnp.dot(attended, out_weight, preferred_element_type=jnp.float32...  19.4 us
  transfers between devices with their start and end apart: 1, of which 1 were waited for; matrix products, arithmetic and copies ran while one was open for 0% of the time, Pallas kernels for 0%

commit v1 on v0

--- a/solution.py
+++ b/solution.py
@@ -6,6 +6,12 @@
 
 HEAD_DIM = 128
 key_block = 512
+
+
+def summed_here(x, axis):
+    parts = lax.all_gather(x, axis, axis=0, tiled=False)
+    acc = parts.sum(axis=0)
+    return acc
 
 
 def rope_angles(row_pos, col_pos, head_dim):
@@ -122,7 +128,7 @@
     attended = (
         (accumulated / row_total.T[:, :, None]).astype(jnp.bfloat16).reshape(local_tokens, features)
     )
-    projected = lax.psum(
+    projected = summed_here(
         jnp.dot(attended, out_weight, preferred_element_type=jnp.float32).astype(jnp.bfloat16),
         "tensor",
     ).astype(jnp.float32)

time: 192 us -> 158 us (0.82)
  waiting for transfers between devices: 19.4 us -> 0 us
  between operations: 13.6 us -> 0.28 us
  other arithmetic: 13.3 us -> 9.89 us
  blocking collectives: 125 us -> 128 us
  matrix products: 7.08 us -> 4.57 us
  local copies, waits for them, and re-layouts: 12.9 us -> 15.4 us
    psum x1 -> x0, waiting for transfers between devices: 19.4 us -> none  [local(): lax.psum(jnp.dot(attended, out_weight, preferred_element_type=jnp.float32...]
    all_gather x0 -> x1, blocking collectives: none -> 2.37 us  [summed_here(): parts = lax.all_gather(x, axis, axis=0, tiled=False)]
    unnamed x21 -> x23, local copies, waits for them, and re-layouts: 3.42 us -> 5.64 us
  transfers between devices with their start and end apart: 1 -> 0, of which waited for: 1 -> 0; matrix products, arithmetic and copies ran while one was open for 0% -> 0% of each run, Pallas kernels for 0% -> 0%
where the time goes in v1:
time: 158 us
  blocking collectives  128 us (81%)
  local copies, waits for them, and re-layouts  15.4 us (10%)
  other arithmetic  9.89 us (6%)
  matrix products  4.57 us (3%)
    all_gather x1, blocking collectives, local(): lax.all_gather(short_keys, 'seq', axis=0, tiled=True)  32.8 us
    all_gather x1, blocking collectives, local(): lax.all_gather(short_values, 'seq', axis=0, tiled=True)  31 us
    all_gather x1, blocking collectives, local(): lax.all_gather(text_keys, 'seq', axis=0, tiled=True)  30.8 us
    all_gather x1, blocking collectives, local(): lax.all_gather(text_values, 'seq', axis=0, tiled=True)  30.8 us
    unnamed x23, local copies, waits for them, and re-layouts  5.64 us
    add x1, other arithmetic, compress(): grid_cells[0, :, 0] * tap_grid[0, 0] + grid_cells[0, :, 1] * tap_grid[0, 1]  3.48 us

profile of v1, /device:TPU:0, one launch (start us, length us, event | category | flops | bytes accessed | tf_op | source)
XLA Modules:
  0.0 157.8 jit_solution(3511188058106103889)
XLA Ops:
  0.0 0.9 reshape.261
  0.9 0.8 mul.304
  1.7 0.8 mul.307
  2.6 0.8 mul.310
  3.4 0.8 mul.313
  4.3 1.1 reshape.259
  5.4 1.0 fusion.27
  6.5 1.1 copy.63
  7.6 1.8 %copy.64 = f32[1,32,1,768]{1,3,2,0:T(8,128)} copy(f32[1,32,1,768]{3,2,1,0:T(1,128)} %get-tuple-element.17) | data formatting | bytes 196608
  9.4 1.8 %copy.65 = f32[1,32,1,768]{1,3,2,0:T(8,128)} copy(f32[1,32,1,768]{3,2,1,0:T(1,128)} %get-tuple-element.16) | data formatting | bytes 196608
  11.2 3.5 %multiply_add_fusion = f32[32,6,64,2]{0,3,2,1:T(2,128)S(1)} fusion(f32[32,6,64,2]{0,3,2,1:T(2,128)S(1)} %bitcast.88, f32[32,6,64,2]{0,3,2,1:T(2,128)} %bitcast.91, f32[32,6,64,2]{0,3,2,1:T(2,128)} %bitcast.90, f32[32,6,64,2]{0,3,2,1:T(2,128)S(1)} %bitcast.89, f32[6,64,2]{2,1,0:T(8,128)} %mul.313, f32[6,64,2]{2,1,0:T(8,128)} %mul.310, f32[6,64,2]{2,1,0:T(8,128)} %mul.307, ...), kind=kLoop, calls=%fused_computation.13 | loop fusion | flops 172032 | bytes 503808 | tf_op jit(solution)/shard_map/add | solution.py:46
  15.0 0.5 subtract_convert_fusion
  15.6 0.5 pad_maximum_fusion.1
  16.2 32.8 %all_gather.20 = bf16[256,768]{1,0:T(8,128)(2,1)S(1)} all-gather(bf16[32,768]{1,0:T(8,128)(2,1)S(1)} %copy.51), channel_id=1, replica_groups=mesh['groups'=2,'seq'=8,'tensor'=2] {'seq'}, dimensions={0}, use_global_device_ids=true | all-gather | bytes 442368 | tf_op jit(solution)/shard_map/all_gather | solution.py:124
  49.0 0.9 copy.52
  50.5 0.5 subtract_convert_fusion.1
  51.0 0.5 pad_maximum_fusion
  51.5 1.4 fusion.30
  52.9 30.8 %all-gather.1 = bf16[8,4,768]{2,1,0:T(4,128)(2,1)S(1)} all-gather(bf16[1,4,768]{2,1,0:T(4,128)(2,1)S(1)} %bitcast.95), channel_id=1, replica_groups=mesh['groups'=2,'seq'=8,'tensor'=2] {'seq'}, dimensions={0}, use_global_device_ids=true | all-gather | bytes 55296 | tf_op jit(solution)/shard_map/all_gather | solution.py:118
  83.9 0.6 copy-done.1
  84.5 0.3 convert_reduce_fusion
  84.9 0.6 bitcast_add_fusion
  85.5 1.1 reshape.263
  86.9 0.7 fusion.8
  87.6 31.0 %all_gather.21 = bf16[256,768]{1,0:T(8,128)(2,1)S(1)} all-gather(bf16[32,768]{1,0:T(8,128)(2,1)S(1)} %fusion.8), channel_id=1, replica_groups=mesh['groups'=2,'seq'=8,'tensor'=2] {'seq'}, dimensions={0}, use_global_device_ids=true | all-gather | bytes 442368 | tf_op jit(solution)/shard_map/all_gather | solution.py:125
  118.6 0.9 copy.58
  119.5 1.3 convolution_bitcast_fusion.1
  120.9 30.8 %all-gather.2 = bf16[8,4,768]{2,1,0:T(4,128)(2,1)S(1)} all-gather(bf16[1,4,768]{2,1,0:T(4,128)(2,1)S(1)} %bitcast.96), channel_id=1, replica_groups=mesh['groups'=2,'seq'=8,'tensor'=2] {'seq'}, dimensions={0}, use_global_device_ids=true | all-gather | bytes 55296 | tf_op jit(solution)/shard_map/all_gather | solution.py:119
  151.7 1.2 fusion.4
  152.9 0.5 convolution_convert_fusion
  153.4 2.4 %all-gather = bf16[256,1536]{1,0:T(8,128)(2,1)S(1)} all-gather(bf16[128,1536]{1,0:T(8,128)(2,1)S(1)} %convolution_convert_fusion), channel_id=2, replica_groups=mesh['groups'=2,'seq'=8,'tensor'=2] {'tensor'}, dimensions={0}, use_global_device_ids=true | all-gather | bytes 1179648 | tf_op jit(solution)/shard_map/all_gather | solution.py:12
  155.9 1.9 %add_convert_fusion = bf16[128,1536]{1,0:T(8,128)(2,1)} fusion(bf16[128,1536]{1,0:T(8,128)(2,1)S(1)} %reduce_sum.38, bf16[128,1536]{1,0:T(8,128)(2,1)} %param.16, f32[1536]{0:T(1024)S(1)} %convert_element_type.79), kind=kLoop, calls=%fused_computation.10 | loop fusion | flops 983040 | bytes 1185792 | tf_op jit(solution)/shard_map/convert_element_type | solution.py:137
  (40 shorter events, 2.0 us)
Async XLA Ops:
  0.0 152.9 %copy-start = (bf16[768,1536]{1,0:T(8,128)(2,1)S(1)}, bf16[768,1536]{1,0:T(8,128)(2,1)}, u32[]{:S(2)}) copy-start(bf16[768,1536]{1,0:T(8,128)(2,1)} %param.15) | copy-start | bytes 7077892
  0.9 2.5 %copy-start.3 = (f32[768]{0:T(1024)}, f32[768]{0:T(1024)S(1)}, u32[]{:S(2)}) copy-start(f32[768]{0:T(1024)S(1)} %get-tuple-element.8) | copy-start | bytes 9220
  14.7 35.5 %copy-start.2 = (bf16[128,768]{1,0:T(8,128)(2,1)S(1)}, bf16[128,768]{1,0:T(8,128)(2,1)}, u32[]{:S(2)}) copy-start(bf16[128,768]{1,0:T(8,128)(2,1)} %param.9) | copy-start | bytes 589828
  49.0 3.9 %copy-start.6 = (bf16[4,768]{1,0:T(4,128)(2,1)S(1)}, bf16[4,768]{1,0:T(4,128)(2,1)}, u32[]{:S(2)}) copy-start(bf16[4,768]{1,0:T(4,128)(2,1)} %param.12) | copy-start | bytes 18436
  83.9 0.6 copy-start.1
  83.9 0.6 copy-start.4
  87.6 33.3 %copy-start.7 = (bf16[4,768]{1,0:T(4,128)(2,1)S(1)}, bf16[4,768]{1,0:T(4,128)(2,1)}, u32[]{:S(2)}) copy-start(bf16[4,768]{1,0:T(4,128)(2,1)} %param.13) | copy-start | bytes 18436
  87.6 64.1 %copy-start.5 = (f32[6,128]{1,0:T(8,128)S(1)}, f32[6,128]{1,0:T(8,128)}, u32[]{:S(2)}) copy-start(f32[6,128]{1,0:T(8,128)} %copy-done.4) | copy-start | bytes 9220
  152.9 3.0 %copy-start.8 = (bf16[1536]{0:T(1024)(128)(2,1)S(1)}, bf16[1536]{0:T(1024)(128)(2,1)}, u32[]{:S(2)}) copy-start(bf16[1536]{0:T(1024)(128)(2,1)} %param.17) | copy-start | bytes 9220
